TPU v7x, 128 devices: a whole 4x4x4 slice. The times are simulated.
128 devices in a mesh: ctx: 32 (over z_lo, y, x), head: 4 (over z_hi, core).
Axes of the slice: x: 4, y: 4, z: 4 (z_hi: 2, z_lo: 2; z = z_hi * 2 + z_lo), core: 2. Of those that a mesh axis runs over, the one named last changes fastest.
Arguments:
- queries: bfloat16 [1024, 16384], P('ctx', 'head'), may hold values from -512 to 512
- kv_cache: bfloat16 [2, 16384, 1024], P(None, 'ctx', 'head'), may hold values from -7 to 7
- fill_len: int32 [32], P('ctx'), may hold values from 64 to 512
- prompt_offset: int32 [1], replicated, may hold values from 8192 to 15360
Outputs:
- attended: bfloat16 [1024, 16384], P(('ctx', 'head'))
All inputs are finite; a program needn't handle non-finite values.
Results may differ from a plain program's by a relative error of at most 0.0045.
Values may be sent and summed in bfloat16 or wider, within the bound.
No kernel may reach another device: no remote copies, remote signals or barrier semaphores. Data moves between devices by JAX's collectives and lax.ppermute only.
A program may use at most 192 MiB of HBM per device.

v0:
```python
import math

import jax
import jax.numpy as jnp
from jax import lax
from jax.sharding import PartitionSpec as P

HEAD_DIM = 128


def shard_partial(query_rows, key_block, value_block, allowed):
    scaling = 1.0 / math.sqrt(query_rows.shape[-1])
    scores = (
        jnp.einsum("nhgd,khd->hgnk", query_rows, key_block, preferred_element_type=jnp.float32)
        * scaling
    )
    scores = jnp.where(allowed[None, None], scores, -1e30)
    row_max = jnp.max(scores, axis=-1)
    weights = jnp.exp(scores - row_max[..., None])
    row_sum = jnp.sum(weights, axis=-1)
    rounded = weights.astype(jnp.bfloat16)
    weighted = jnp.einsum(
        "hgnk,khd->nhgd", rounded, value_block, preferred_element_type=jnp.float32
    )
    weighted = weighted / jnp.transpose(row_sum, (2, 0, 1))[..., None]
    row_count = query_rows.shape[0]
    partial_value = weighted.astype(jnp.bfloat16).reshape(row_count, -1)
    log_total = jnp.transpose(row_max + jnp.log(row_sum), (2, 0, 1)).reshape(row_count, -1)
    return (partial_value, log_total)


def per_device(queries, kv_cache, fill_len, prompt_offset):
    ctx_size = lax.axis_size("ctx")
    ctx_rank = lax.axis_index("ctx")
    slots = kv_cache.shape[1]
    kv_local = kv_cache.shape[2] // HEAD_DIM
    feat_width = queries.shape[1]
    heads_local = feat_width // HEAD_DIM
    groups = heads_local // kv_local
    slot_ids = jnp.arange(slots, dtype=jnp.int32)
    start_pos = prompt_offset[0]
    key_block = kv_cache[0].reshape(slots, kv_local, HEAD_DIM)
    value_block = kv_cache[1].reshape(slots, kv_local, HEAD_DIM)
    key_pos = ctx_rank * slots + slot_ids
    live_slots = slot_ids < fill_len[0]
    arrived = lax.all_gather(queries, "ctx", axis=0, tiled=True)
    row_count = arrived.shape[0]
    query_pos = start_pos + jnp.arange(row_count, dtype=jnp.int32)
    allowed = live_slots[None, :] & (key_pos[None, :] <= query_pos[:, None])
    partial_value, log_total = shard_partial(
        arrived.reshape(row_count, kv_local, groups, HEAD_DIM), key_block, value_block, allowed
    )
    received = lax.all_to_all(
        partial_value[None], ("ctx", "head"), split_axis=1, concat_axis=0, tiled=True
    )
    received_logs = lax.all_to_all(
        log_total[None], ("ctx", "head"), split_axis=1, concat_axis=0, tiled=True
    )
    head_size = lax.axis_size("head")
    token_rows = received.shape[1]
    received = received.reshape(ctx_size, head_size, token_rows, heads_local, HEAD_DIM)
    received_logs = received_logs.reshape(ctx_size, head_size, token_rows, heads_local)
    log_peak = jnp.max(received_logs, axis=0)
    shares = jnp.exp(received_logs - log_peak[None])
    merged = (
        jnp.sum(shares[..., None] * received.astype(jnp.float32), axis=0)
        / jnp.sum(shares, axis=0)[..., None]
    )
    merged = jnp.transpose(merged, (1, 0, 2, 3)).reshape(token_rows, head_size * feat_width)
    return merged.astype(jnp.bfloat16)


def solution(mesh):
    in_specs = (P("ctx", "head"), P(None, "ctx", "head"), P("ctx"), P())
    out_specs = P(("ctx", "head"), None)
    return jax.shard_map(
        per_device, mesh=mesh, in_specs=in_specs, out_specs=out_specs, check_vma=False
    )
```

profile of v0, /device:TPU:12, one launch (start us, length us, event | category | flops | bytes accessed | tf_op | source)
XLA Modules:
  0.0 589.1 jit_solution(6618123651662183194)
XLA Ops:
  6.5 0.0 all-gather.2.cloned.1.call-start
  6.5 0.7 all-gather.2.cloned.1.call-update
  8.5 1.1 fusion.13
  9.6 0.1 copy.46
  9.8 0.1 copy.36
  9.9 0.4 compare_and_fusion
  10.4 158.9 %all-gather.2.cloned.1.call-done = bf16[1024,4096]{1,0:T(8,128)(2,1)} async-done(((bf16[32,4096]{1,0:T(8,128)(2,1)}), bf16[1024,4096]{1,0:T(8,128)(2,1)}) %all-gather.2.cloned.1.call-update) | async-done | bytes 8388624 | tf_op jit(solution)/shard_map/all_gather | solution.py:46
  169.3 12.0 %copy.32 = bf16[1024,4096]{0,1:T(8,128)(2,1)} copy(bf16[1024,4096]{1,0:T(8,128)(2,1)} %all-gather.2.cloned.1.call-done) | data formatting | bytes 16777216 | tf_op jit(solution)/shard_map/all_gather | solution.py:46
  181.3 28.0 %fusion.2 = (f32[2,16,1024]{2,1,0:T(8,128)S(1)}, f32[2,512,1024,16]{2,1,3,0:T(8,128)}) fusion(pred[1024,512]{0,1:T(8,128)(4,1)S(1)} %compare_and_fusion, bf16[512,2,128,1]{0,2,3,1:T(8,128)(2,1)S(1)} %bitcast.63, bf16[1024,2,16,128]{0,3,2,1:T(8,128)(2,1)} %bitcast.58), kind=kOutput, calls=%fused_computation.4 | convolution fusion | flops 4345266176 | bytes 76414976 | tf_op jit(solution)/shard_map/nhgd,khd->hgnk/dot_general | solution.py:14
  209.3 21.6 %fusion.1 = f32[2,16,1024]{2,1,0:T(8,128)S(1)} fusion(f32[2,512,1024,16]{2,1,3,0:T(8,128)} %get-tuple-element.10, f32[2,16,1024]{2,1,0:T(8,128)S(1)} %get-tuple-element.9, pred[1024,512]{0,1:T(8,128)(4,1)S(1)} %compare_and_fusion), kind=kLoop, calls=%fused_computation.3 | loop fusion | flops 67076096 | bytes 67895296 | tf_op jit(solution)/shard_map/reduce_sum | solution.py:20
  230.9 0.3 copy.35
  231.3 0.6 broadcast.68
  231.8 1.9 reduce.1
  233.8 0.9 reshape.98
  234.7 16.7 %all-to-all-start = ((f32[128,1,256]{2,1,0:T(1,128)}), f32[128,1,256]{2,1,0:T(1,128)S(1)}, u32[]{:S(2)}, u32[]{:S(2)}) async-start(f32[128,1,256]{2,1,0:T(1,128)} %reshape.98), calls=%async_computation | async-start | bytes 262144 | tf_op jit(solution)/shard_map/all_to_all | solution.py:56
  251.4 28.0 %fusion.6 = bf16[1024,2,16,128]{0,3,2,1:T(8,128)(2,1)} fusion(f32[1024,2,16]{0,2,1:T(8,128)S(1)} %bitcast.65, bf16[512,2,128,1]{0,2,3,1:T(8,128)(2,1)S(1)} %bitcast.67, f32[2,512,1024,16]{2,1,3,0:T(8,128)} %get-tuple-element.10, f32[2,16,1024]{2,1,0:T(8,128)S(1)} %get-tuple-element.9, pred[1024,512]{0,1:T(8,128)(4,1)S(1)} %compare_and_fusion), kind=kOutput, calls=%fused_computation.8 | convolution fusion | flops 4370464768 | bytes 76546048 | tf_op jit(solution)/shard_map/hgnk,khd->nhgd/dot_general | solution.py:22
  279.5 36.5 %copy.38 = bf16[1,1024,4096]{2,0,1:T(2,128)(2,1)} copy(bf16[1,1024,4096]{1,2,0:T(8,128)(2,1)} %bitcast.59) | data formatting | bytes 16777216 | tf_op jit(solution)/shard_map/broadcast_in_dim;reshape | solution.py:54
  316.0 0.5 broadcast.67
  316.5 52.4 %reduce = bf16[1024,4096]{1,0:T(8,128)(2,1)} reduce(bf16[1024,1,4096]{2,1,0:T(2,128)(2,1)} %bitcast.56, bf16[]{:T(256)} %broadcast.67), dimensions={1}, to_apply=%bitcast.45.reduce_sub_computation | reduce | bytes 16777218
  369.0 15.7 %reshape.96 = bf16[128,2,16384]{2,1,0:T(2,128)(2,1)} reshape(bf16[1024,4096]{1,0:T(8,128)(2,1)} %reduce) | data formatting | bytes 16777216
  384.7 0.0 all-to-all-done
  384.7 10.2 %all-to-all-start.1 = ((bf16[128,2,16384]{2,1,0:T(2,128)(2,1)}), bf16[128,2,16384]{2,1,0:T(2,128)(2,1)}, u32[]{:S(2)}, u32[]{:S(2)}) async-start(bf16[128,2,16384]{2,1,0:T(2,128)(2,1)} %reshape.96), calls=%async_computation.1 | async-start | bytes 16777216 | tf_op jit(solution)/shard_map/all_to_all | solution.py:53
  394.9 0.9 reduce.2
  395.8 0.9 reshape.99
  396.8 0.1 reduce_max.22
  396.8 0.1 fusion.12
  396.9 121.9 %all-to-all-done.1 = bf16[128,2,16384]{2,1,0:T(2,128)(2,1)} async-done(((bf16[128,2,16384]{2,1,0:T(2,128)(2,1)}), bf16[128,2,16384]{2,1,0:T(2,128)(2,1)}, u32[]{:S(2)}, u32[]{:S(2)}) %all-to-all-start.1) | async-done | bytes 8388640 | tf_op jit(solution)/shard_map/all_to_all | solution.py:53
  518.8 38.4 %reshape.97 = bf16[1024,1,4096]{2,1,0:T(2,128)(2,1)} reshape(bf16[128,2,16384]{2,1,0:T(2,128)(2,1)} %all-to-all-done.1) | data formatting | bytes 16777216
  557.2 18.9 %bitcast_convert_fusion = f32[1,1024,4096]{2,0,1:T(1,128)S(1)} fusion(bf16[1024,1,4096]{2,1,0:T(2,128)(2,1)} %reshape.97), kind=kLoop, calls=%fused_computation.23 | loop fusion | flops 4194304 | bytes 25165824 | tf_op jit(solution)/shard_map/convert_element_type | solution.py:66
  576.1 5.1 multiply_reduce_fusion
  581.1 0.2 fusion.9
  581.4 0.9 copy.49
  (5 shorter events, 0.1 us)
Async XLA Ops:
  6.5 162.8 %all-gather.2.cloned.1.call-start = ((), (), s32[]{:S(2)}) async-start(), calls=%async_computation.2 | async-start | bytes 8650752 | tf_op jit(solution)/shard_map/all_gather | solution.py:46
  234.7 150.0 %all-to-all-start = ((f32[128,1,256]{2,1,0:T(1,128)}), f32[128,1,256]{2,1,0:T(1,128)S(1)}, u32[]{:S(2)}, u32[]{:S(2)}) async-start(f32[128,1,256]{2,1,0:T(1,128)} %reshape.98), calls=%async_computation | async-start | bytes 262144 | tf_op jit(solution)/shard_map/all_to_all | solution.py:56
  384.7 134.1 %all-to-all-start.1 = ((bf16[128,2,16384]{2,1,0:T(2,128)(2,1)}), bf16[128,2,16384]{2,1,0:T(2,128)(2,1)}, u32[]{:S(2)}, u32[]{:S(2)}) async-start(bf16[128,2,16384]{2,1,0:T(2,128)(2,1)} %reshape.96), calls=%async_computation.1 | async-start | bytes 16777216 | tf_op jit(solution)/shard_map/all_to_all | solution.py:53
Sparse Core Ops, SparseCore 0:
  9.0 160.2 all-gather.1
where the time goes:
time: 592 us; the launch traced here: 589 us
  waiting for transfers between devices  282 us (48%)
  local copies, waits for them, and re-layouts  108 us (18%)
  other arithmetic  102 us (17%)
  matrix products  56 us (9%)
  starting transfers between devices  27 us (5%)
  between operations  14.8 us (2%)
    all_gather x1, waiting for transfers between devices, per_device(): arrived = lax.all_gather(queries, 'ctx', axis=0, tiled=True)  159 us
    all_to_all x1, waiting for transfers between devices, per_device(): lax.all_to_all(partial_value[None], ('ctx', 'head'), split_axis=1, concat...  122 us
    unnamed x8, local copies, waits for them, and re-layouts  58 us
    unnamed x2, other arithmetic  54.4 us
    another operation x1, local copies, waits for them, and re-layouts, per_device(): partial_value[None]  36.5 us
    dot_general x1, matrix products, shard_partial(): jnp.einsum('hgnk,khd->nhgd', rounded, value_block, preferred_element_type...  28 us
    dot_general x1, matrix products, shard_partial(): jnp.einsum('nhgd,khd->hgnk', query_rows, key_block, preferred_element_typ...  28 us
    reduce_sum x1, other arithmetic, shard_partial(): row_sum = jnp.sum(weights, axis=-1)  21.6 us
  transfers between devices with their start and end apart: 3, of which 2 were waited for; matrix products, arithmetic and copies ran while one was open for 23% of the time, Pallas kernels for 0%

commit v1 on v0

v1 whole, which is shorter than its diff:
```python
import functools
import math

import jax
import jax.numpy as jnp
from jax import lax
from jax.experimental import pallas as pl
from jax.experimental.pallas import tpu as pltpu
from jax.sharding import Mesh, PartitionSpec as P


HEAD_DIM = 128
SLOTS = 512
WIDTH = 512
SCALING = 1.0 / math.sqrt(HEAD_DIM)
LOG2E = math.log2(math.e)
MASKED = -1e30
CODE = 2 * SLOTS


def attend_kernel(along, coords, offset_ref, *refs):
    q_refs, kv_refs, out_ref = refs[:4], refs[4:12], refs[12]
    kbuf, vbuf, score0, score1, peak0, peak1, acc, logs, count = refs[13:]
    if coords is None:
        zl, y, x = lax.axis_index("zl"), lax.axis_index("y"), lax.axis_index("x")
    else:
        zl, y, x = coords
    offset = offset_ref[0]
    mine = y if along == "y" else x

    def ctx_of(z, step):
        return z * 16 + (step * 4 + x if along == "y" else y * 4 + step)

    other = x if along == "y" else y
    groups, places = [], []
    for k in range(4):
        g = (other + 4 - k) & 3
        places.append(pl.multiple_of(g * 32, 32))
        groups.append(zl * 16 + (y * 4 + g if along == "y" else g * 4 + x))
    first_token = offset + (zl * 16 + (y * 4 if along == "y" else x)) * 32
    last_token = first_token + 31 + (3 * 32 if along == "y" else 12 * 32)

    shard, fill, room = [], [], []
    for k in range(8):
        j = ctx_of(zl if k < 4 else 1 - zl, (mine + 4 - (k & 3)) & 3)
        code = kv_refs[k][CODE : CODE + 16, :].astype(jnp.float32)
        n = jnp.max(code[0:8]).astype(jnp.int32) * 16 + jnp.max(code[8:16]).astype(jnp.int32)
        n = jnp.where(j * SLOTS > last_token, 0, n)
        shard.append(j)
        fill.append(n)
        room.append(((n + 15) >> 4) << 4)
    start = []
    for k in range(8):
        before = jnp.int32(0)
        for o in range(8):
            if o != k:
                before = before + jnp.where(shard[o] < shard[k], room[o], 0)
        start.append(before)
    total = functools.reduce(lambda a, b: a + b, room)

    row = lax.broadcasted_iota(jnp.int32, (SLOTS, HEAD_DIM), 0)
    ones = jnp.ones((SLOTS, HEAD_DIM), jnp.bfloat16)
    zeros = jnp.zeros((SLOTS, HEAD_DIM), jnp.bfloat16)

    def pack(k):
        live = row < fill[k]
        at = pl.ds(pl.multiple_of(start[k], 16), SLOTS)
        keys = kv_refs[k][0:SLOTS, :]
        kbuf[at, :] = jnp.where(live, keys, jnp.broadcast_to(kv_refs[k][0:1, :], keys.shape))
        vbuf[at, 0:HEAD_DIM] = jnp.where(live, kv_refs[k][SLOTS : 2 * SLOTS, :], zeros)
        vbuf[at, HEAD_DIM:] = jnp.where(live, ones, zeros)

    for half in range(2):
        for step in range(4):
            for k in range(8):
                is_half = (zl if k < 4 else 1 - zl) == half
                is_step = ((mine + 4 - (k & 3)) & 3) == step
                pl.when(is_half & is_step & (fill[k] > 0))(functools.partial(pack, k))
    rest = pl.ds(pl.multiple_of(total, 16), WIDTH)
    kbuf[rest, :] = zeros
    vbuf[rest, 0:HEAD_DIM] = zeros
    vbuf[rest, HEAD_DIM:] = zeros

    token = lax.broadcasted_iota(jnp.int32, (32, HEAD_DIM), 0)
    for i in range(4):
        position = offset + groups[i] * 32 + token
        seen = jnp.zeros((32, HEAD_DIM), jnp.int32)
        for k in range(8):
            seen = seen + jnp.clip(position + 1 - shard[k] * SLOTS, 0, room[k])
        count[32 * i : 32 * i + 32, :] = seen
        count[128 + 32 * i : 160 + 32 * i, :] = seen
    least = jnp.int32(0)
    for k in range(8):
        least = least + jnp.clip(first_token + 1 - shard[k] * SLOTS, 0, room[k])
    clear = least // WIDTH
    blocks = (total + WIDTH - 1) // WIDTH
    logs[...] = jnp.zeros_like(logs)
    lane = lax.broadcasted_iota(jnp.int32, (256, HEAD_DIM), 1)
    lane_half = lax.broadcasted_iota(jnp.int32, (128, HEAD_DIM), 1)

    def queries_of(p):
        parts = []
        for h in range(2):
            cols = pl.ds(pl.multiple_of((2 * p + h) * HEAD_DIM, HEAD_DIM), HEAD_DIM)
            parts += [ref[:, cols] for ref in q_refs]
        return jnp.concatenate(parts, axis=0)

    def score(query, b, scores, peak, masked):
        at = pl.ds(pl.multiple_of(b * WIDTH, WIDTH), WIDTH)
        value = lax.dot_general(query, kbuf[at, :], (((1,), (1,)), ((), ())), preferred_element_type=jnp.float32)
        tiles = [value[:, 128 * t : 128 * t + 128] for t in range(WIDTH // 128)]
        if masked:
            limit = count[...] - b * WIDTH
            tiles = [jnp.where(lane + 128 * t < limit, tile, MASKED) for t, tile in enumerate(tiles)]
        top = peak[...]
        for t, tile in enumerate(tiles):
            scores[b, :, 128 * t : 128 * t + 128] = tile
            top = jnp.maximum(top, tile)
        peak[...] = top

    def weigh(b, scores, peak):
        at = pl.ds(pl.multiple_of(b * WIDTH, WIDTH), WIDTH)
        top = peak[...]
        weights = [
            jnp.exp2((scores[b, :, 128 * t : 128 * t + 128] - top) * (SCALING * LOG2E)).astype(jnp.bfloat16)
            for t in range(WIDTH // 128)
        ]
        acc[...] += jnp.dot(jnp.concatenate(weights, axis=1), vbuf[at, :], preferred_element_type=jnp.float32)

    def settle(peak):
        peak[...] = jnp.broadcast_to(jnp.max(peak[...], axis=1, keepdims=True), (256, HEAD_DIM))

    def finish(p, peak):
        mass = acc[:, HEAD_DIM:]
        partial = (acc[:, 0:HEAD_DIM] / mass).astype(jnp.bfloat16)
        log_total = peak[...] * SCALING + jnp.log(mass)
        for h in range(2):
            cols = pl.ds(pl.multiple_of((2 * p + h) * HEAD_DIM, HEAD_DIM), HEAD_DIM)
            for i in range(4):
                lo = 128 * h + 32 * i
                out_ref[pl.ds(places[i], 32), cols] = partial[lo : lo + 32]
            logs[...] = jnp.where(lane_half == 2 * p + h, log_total[128 * h : 128 * h + 128], logs[...])

    def stage(p, new, old):
        if new is not None:
            new[1][...] = jnp.full((256, HEAD_DIM), MASKED, jnp.float32)
            query = queries_of(p)
        if old is not None:
            acc[...] = jnp.zeros_like(acc)

        def body(b, masked):
            if old is not None:
                weigh(b, *old)
            if new is not None:
                score(query, b, *new, masked)

        def plain(b, c):
            body(b, False)
            return c

        def edged(b, c):
            body(b, True)
            return c

        if new is None:
            lax.fori_loop(0, blocks, plain, 0)
        else:
            lax.fori_loop(0, clear, plain, 0)
            lax.fori_loop(clear, blocks, edged, 0)
            settle(new[1])
        if old is not None:
            finish(p - 1, old[1])

    first, second = (score0, peak0), (score1, peak1)
    stage(0, first, None)

    def two(i, c):
        stage(2 * i + 1, second, first)
        stage(2 * i + 2, first, second)
        return c

    lax.fori_loop(0, 3, two, 0)
    stage(7, second, first)
    stage(8, None, second)

    value = logs[...]
    high = value.astype(jnp.bfloat16).astype(jnp.float32)
    left = value - high
    middle = left.astype(jnp.bfloat16).astype(jnp.float32)
    low = (left - middle).astype(jnp.bfloat16).astype(jnp.float32)
    packed = (high + pltpu.roll(middle, 32, 1) + pltpu.roll(low, 64, 1)).astype(jnp.bfloat16)
    for i in range(4):
        out_ref[pl.ds(places[i], 32), 2048:2176] = packed[32 * i : 32 * i + 32]


def attend(along, offset, q_pieces, kv_pieces, coords=None):
    room = 8 * SLOTS
    return pl.pallas_call(
        functools.partial(attend_kernel, along, coords),
        out_shape=jax.ShapeDtypeStruct((128, 2176), jnp.bfloat16),
        in_specs=[pl.BlockSpec(memory_space=pltpu.SMEM)] + [pl.BlockSpec(memory_space=pltpu.VMEM)] * 12,
        out_specs=pl.BlockSpec(memory_space=pltpu.VMEM),
        scratch_shapes=[
            pltpu.VMEM((room + WIDTH, HEAD_DIM), jnp.bfloat16),
            pltpu.VMEM((room + WIDTH, 2 * HEAD_DIM), jnp.bfloat16),
            pltpu.VMEM((room // WIDTH, 256, WIDTH), jnp.float32),
            pltpu.VMEM((room // WIDTH, 256, WIDTH), jnp.float32),
            pltpu.VMEM((256, HEAD_DIM), jnp.float32),
            pltpu.VMEM((256, HEAD_DIM), jnp.float32),
            pltpu.VMEM((256, 2 * HEAD_DIM), jnp.float32),
            pltpu.VMEM((128, HEAD_DIM), jnp.float32),
            pltpu.VMEM((256, HEAD_DIM), jnp.int32),
        ],
    )(offset, *q_pieces, *kv_pieces)


def merge_kernel(first_ref, second_ref, out_ref):
    for side, in_ref in enumerate((first_ref, second_ref)):
        totals = []
        for s in range(4):
            code = in_ref[s, 0, :, 2048:2176].astype(jnp.float32)
            totals.append(code + pltpu.roll(code, 96, 1) + pltpu.roll(code, 64, 1))
        peak = functools.reduce(jnp.maximum, totals)
        shares = [jnp.exp(t - peak) for t in totals]
        mass = shares[0] + shares[1] + shares[2] + shares[3]
        shares = [s / mass for s in shares]
        for h in range(16):
            cols = slice(h * HEAD_DIM, (h + 1) * HEAD_DIM)
            total = jnp.zeros((8, HEAD_DIM), jnp.float32)
            for s in range(4):
                share = jnp.broadcast_to(shares[s][:, h : h + 1], (8, HEAD_DIM))
                total = total + share * in_ref[s, 0, :, cols].astype(jnp.float32)
            at = side * 2048 + h * HEAD_DIM
            out_ref[:, at : at + HEAD_DIM] = total.astype(jnp.bfloat16)


def merge(first, second):
    block = pl.BlockSpec((4, 1, 8, 2176), lambda g: (0, g, 0, 0))
    return pl.pallas_call(
        merge_kernel,
        grid=(4,),
        out_shape=jax.ShapeDtypeStruct((8, 16384), jnp.bfloat16),
        in_specs=[block, block],
        out_specs=pl.BlockSpec((8, 4096), lambda g: (0, g)),
        name="merge",
    )(first, second)


def shift(value, axis, by):
    size = lax.axis_size(axis)
    return lax.ppermute(value, axis, [(i, (i + by) % size) for i in range(size)])


def per_device(queries, kv_cache, fill_len, prompt_offset):
    fill = fill_len[0]
    code = jnp.concatenate(
        [jnp.full((8, HEAD_DIM), fill // 16, jnp.bfloat16), jnp.full((8, HEAD_DIM), fill % 16, jnp.bfloat16)], axis=0
    )
    parts = []
    for part, (along, other) in enumerate((("y", "x"), ("x", "y"))):
        cols = slice(part * HEAD_DIM, (part + 1) * HEAD_DIM)
        cache = jnp.concatenate([kv_cache[0, :, cols], kv_cache[1, :, cols], code], axis=0)
        query = queries[:, part * 2048 : (part + 1) * 2048]

        across = shift(cache, "zl", 1)
        q_pieces = [query] + [shift(query, other, k) for k in (1, 2, 3)]
        kv_pieces = [cache] + [shift(cache, along, k) for k in (1, 2, 3)]
        kv_pieces += [across] + [shift(across, along, k) for k in (1, 2, 3)]
        parts.append((along, other, q_pieces, kv_pieces))
    received = []
    for along, other, q_pieces, kv_pieces in parts:
        partial = attend(along, prompt_offset, q_pieces, kv_pieces)
        swapped = lax.all_to_all(
            partial.reshape(16, 8, 2176), (other, "zh", "core"), split_axis=0, concat_axis=0, tiled=True
        )
        received.append(swapped.reshape(4, 4, 8, 2176))
    return merge(*received)


def solution(mesh):
    split = Mesh(mesh.devices.reshape(2, 4, 4, 2, 2), ("zl", "y", "x", "zh", "core"))
    ctx, head = ("zl", "y", "x"), ("zh", "core")
    return jax.shard_map(
        per_device,
        mesh=split,
        in_specs=(P(ctx, head), P(None, ctx, head), P(ctx), P()),
        out_specs=P(ctx + head, None),
        check_vma=False,
    )
```

time: 592 us -> 138 us (0.23)
  the two profiles are of different devices: /device:TPU:12 before, /device:TPU:1 now
where the time goes in v1:
time: 138 us; the launch traced here: 137 us
  Pallas kernels  36.4 us (26%)
  starting transfers between devices  36.3 us (26%)
  waiting for transfers between devices  35 us (25%)
  blocking collectives  24.8 us (18%)
  local copies, waits for them, and re-layouts  2.74 us (2%)
  between operations  1.6 us (1%)
    ppermute x20, waiting for transfers between devices, shift(): lax.ppermute(value, axis, [(i, (i + by) % size) for i in range(size)])  35 us
    pallas_call x2, Pallas kernels, attend(): pl.pallas_call(functools.partial(attend_kernel, along, coords), out_shape...  32.5 us
    ppermute x20, starting transfers between devices, shift(): lax.ppermute(value, axis, [(i, (i + by) % size) for i in range(size)])  28.8 us
    all_to_all x1, blocking collectives, per_device(): lax.all_to_all(partial.reshape(16, 8, 2176), (other, 'zh', 'core'), split...  24.8 us
    all_to_all x1, starting transfers between devices, per_device(): lax.all_to_all(partial.reshape(16, 8, 2176), (other, 'zh', 'core'), split...  7.5 us
    pallas_call x1, Pallas kernels, merge(): pl.pallas_call(merge_kernel, grid=(4,), out_shape=jax.ShapeDtypeStruct((8...  3.94 us
  transfers between devices with their start and end apart: 21, of which 11 were waited for; matrix products, arithmetic and copies ran while one was open for 0% of the time, Pallas kernels for 24%

profile of v1, /device:TPU:1, one launch (start us, length us, event | category | flops | bytes accessed | tf_op | source)
XLA Modules:
  0.0 137.1 jit_solution(13651587149646798705)
XLA Ops:
  0.7 0.1 pad.7.clone
  0.8 1.1 slice_bitcast_fusion.1
  1.9 0.0 copy-start.19
  1.9 0.3 maximum_maximum_fusion.1
  2.3 2.5 %collective-permute-start.16 = (bf16[1040,128]{1,0:T(8,128)(2,1)S(1)}, bf16[1040,128]{1,0:T(8,128)(2,1)S(1)}, u32[]{:S(2)}, u32[]{:S(2)}) collective-permute-start(bf16[1040,128]{1,0:T(8,128)(2,1)S(1)} %get-tuple-element.11.refs_4_), channel_id=1, source_target_pairs={{0,64},{64,0},{1,65},{65,1},{2,66},{66,2},{3,67},{67,3},{4,68},{68... | collective-permute-start | bytes 798728 | tf_op jit(solution)/shard_map/ppermute | solution.py:251
  4.8 1.2 collective-permute-start.13
  6.1 0.0 copy-start.3
  6.1 1.4 collective-permute-start.10
  7.5 2.6 %collective-permute-start.11 = (bf16[32,2048]{1,0:T(8,128)(2,1)S(1)}, bf16[32,2048]{1,0:T(8,128)(2,1)S(1)}, u32[]{:S(2)}, u32[]{:S(2)}) collective-permute-start(bf16[32,2048]{1,0:T(8,128)(2,1)S(1)} %get-tuple-element.9.refs_0_), channel_id=1, source_target_pairs={{0,32},{16,48},{32,0},{48,16},{1,33},{17,49},{33,1},{49,17},{2,34}... | collective-permute-start | bytes 393224 | tf_op jit(solution)/shard_map/ppermute | solution.py:251
  10.1 1.1 collective-permute-start.12
  11.2 0.4 collective-permute-done.10.refs_1_
  11.6 2.2 %collective-permute-start.14 = (bf16[1040,128]{1,0:T(8,128)(2,1)S(1)}, bf16[1040,128]{1,0:T(8,128)(2,1)S(1)}, u32[]{:S(2)}, u32[]{:S(2)}) collective-permute-start(bf16[1040,128]{1,0:T(8,128)(2,1)S(1)} %get-tuple-element.11.refs_4_), channel_id=1, source_target_pairs={{0,8},{4,12},{8,0},{12,4},{1,9},{5,13},{9,1},{13,5},{2,10},{6,14},... | collective-permute-start | bytes 798728 | tf_op jit(solution)/shard_map/ppermute | solution.py:251
  13.7 1.2 collective-permute-done.11.refs_2_
  14.9 1.5 %collective-permute-start.15 = (bf16[1040,128]{1,0:T(8,128)(2,1)S(1)}, bf16[1040,128]{1,0:T(8,128)(2,1)S(1)}, u32[]{:S(2)}, u32[]{:S(2)}) collective-permute-start(bf16[1040,128]{1,0:T(8,128)(2,1)S(1)} %get-tuple-element.11.refs_4_), channel_id=1, source_target_pairs={{0,12},{4,0},{8,4},{12,8},{1,13},{5,1},{9,5},{13,9},{2,14},{6,2},{... | collective-permute-start | bytes 798728 | tf_op jit(solution)/shard_map/ppermute | solution.py:251
  16.4 0.0 collective-permute-done.16.refs_8_
  16.4 0.0 collective-permute-start.17
  16.4 2.4 %collective-permute-start.18 = (bf16[1040,128]{1,0:T(8,128)(2,1)S(1)}, bf16[1040,128]{1,0:T(8,128)(2,1)S(1)}, u32[]{:S(2)}, u32[]{:S(2)}) collective-permute-start(bf16[1040,128]{1,0:T(8,128)(2,1)S(1)} %collective-permute-done.16.refs_8_), channel_id=1, source_target_pairs={{0,8},{4,12},{8,0},{12,4},{1,9},{5,13},{9,1},{13,5},{2,10},{6,14},... | collective-permute-start | bytes 798728 | tf_op jit(solution)/shard_map/ppermute | solution.py:251
  18.9 0.0 collective-permute-done.13.refs_5_
  18.9 1.2 collective-permute-start.19
  20.0 0.0 collective-permute-done.14.refs_6_
  20.0 0.4 collective-permute-start.6
  20.5 5.1 %collective-permute-done.15.refs_7_ = bf16[1040,128]{1,0:T(8,128)(2,1)S(1)} collective-permute-done((bf16[1040,128]{1,0:T(8,128)(2,1)S(1)}, bf16[1040,128]{1,0:T(8,128)(2,1)S(1)}, u32[]{:S(2)}, u32[]{:S(2)}) %collective-permute-start.15) | collective-permute-done | bytes 266272 | tf_op jit(solution)/shard_map/ppermute | solution.py:251
  26.2 0.2 collective-permute-done.17.refs_9_
  26.4 5.2 %collective-permute-done.18.refs_10_ = bf16[1040,128]{1,0:T(8,128)(2,1)S(1)} collective-permute-done((bf16[1040,128]{1,0:T(8,128)(2,1)S(1)}, bf16[1040,128]{1,0:T(8,128)(2,1)S(1)}, u32[]{:S(2)}, u32[]{:S(2)}) %collective-permute-start.18) | collective-permute-done | bytes 266272 | tf_op jit(solution)/shard_map/ppermute | solution.py:251
  31.6 3.8 %collective-permute-done.19.refs_11_ = bf16[1040,128]{1,0:T(8,128)(2,1)S(1)} collective-permute-done((bf16[1040,128]{1,0:T(8,128)(2,1)S(1)}, bf16[1040,128]{1,0:T(8,128)(2,1)S(1)}, u32[]{:S(2)}, u32[]{:S(2)}) %collective-permute-start.19) | collective-permute-done | bytes 266272 | tf_op jit(solution)/shard_map/ppermute | solution.py:251
  35.5 0.7 copy-done.16
  36.2 19.0 %shard_map.47 = bf16[128,2176]{1,0:T(8,128)(2,1)} custom-call(s32[1]{0:T(128)S(6)} %copy.6.offset_ref, bf16[32,2048]{1,0:T(8,128)(2,1)} %copy-done.4, bf16[32,2048]{1,0:T(8,128)(2,1)} %copy-done.20, bf16[32,2048]{1,0:T(8,128)(2,1)} %copy-done.21, bf16[32,2048]{1,0:T(8,128)(2,1)} %copy-done.22, bf16[1040,128]{1,0:T(8,128)(2,1)} %copy-done.2, ...), custom_call_target="tpu_custom_call" | custom-call | tf_op jit(solution)/shard_map/pallas_call | solution.py:198
  55.2 7.5 %all-to-all-start.1 = ((bf16[16,8,2176]{2,1,0:T(8,128)(2,1)}), bf16[16,8,2176]{2,1,0:T(8,128)(2,1)S(1)}, u32[]{:S(2)}, u32[]{:S(2)}) async-start(bf16[16,8,2176]{2,1,0:T(8,128)(2,1)} %bitcast.17), calls=%async_computation.1 | async-start | bytes 1114112 | tf_op jit(solution)/shard_map/all_to_all | solution.py:273
  62.7 1.9 %collective-permute-start = (bf16[32,2048]{1,0:T(8,128)(2,1)S(1)}, bf16[32,2048]{1,0:T(8,128)(2,1)S(1)}, u32[]{:S(2)}, u32[]{:S(2)}) collective-permute-start(bf16[32,2048]{1,0:T(8,128)(2,1)S(1)} %get-tuple-element.10.refs_0_), channel_id=1, source_target_pairs={{0,4},{4,8},{8,12},{12,0},{1,5},{5,9},{9,13},{13,1},{2,6},{6,10},{... | collective-permute-start | bytes 393224 | tf_op jit(solution)/shard_map/ppermute | solution.py:251
  64.6 1.9 %collective-permute-start.1 = (bf16[32,2048]{1,0:T(8,128)(2,1)S(1)}, bf16[32,2048]{1,0:T(8,128)(2,1)S(1)}, u32[]{:S(2)}, u32[]{:S(2)}) collective-permute-start(bf16[32,2048]{1,0:T(8,128)(2,1)S(1)} %get-tuple-element.10.refs_0_), channel_id=1, source_target_pairs={{0,8},{4,12},{8,0},{12,4},{1,9},{5,13},{9,1},{13,5},{2,10},{6,14},... | collective-permute-start | bytes 393224 | tf_op jit(solution)/shard_map/ppermute | solution.py:251
  66.5 0.8 collective-permute-start.2
  67.3 1.5 %collective-permute-done.refs_1_ = bf16[32,2048]{1,0:T(8,128)(2,1)S(1)} collective-permute-done((bf16[32,2048]{1,0:T(8,128)(2,1)S(1)}, bf16[32,2048]{1,0:T(8,128)(2,1)S(1)}, u32[]{:S(2)}, u32[]{:S(2)}) %collective-permute-start) | collective-permute-done | bytes 131104 | tf_op jit(solution)/shard_map/ppermute | solution.py:251
  68.8 2.6 %collective-permute-start.4 = (bf16[1040,128]{1,0:T(8,128)(2,1)S(1)}, bf16[1040,128]{1,0:T(8,128)(2,1)S(1)}, u32[]{:S(2)}, u32[]{:S(2)}) collective-permute-start(bf16[1040,128]{1,0:T(8,128)(2,1)S(1)} %get-tuple-element.12.refs_4_), channel_id=1, source_target_pairs={{0,32},{16,48},{32,0},{48,16},{1,33},{17,49},{33,1},{49,17},{2,34}... | collective-permute-start | bytes 798728 | tf_op jit(solution)/shard_map/ppermute | solution.py:251
  71.4 1.4 collective-permute-done.1.refs_2_
  72.8 2.3 %collective-permute-start.5 = (bf16[1040,128]{1,0:T(8,128)(2,1)S(1)}, bf16[1040,128]{1,0:T(8,128)(2,1)S(1)}, u32[]{:S(2)}, u32[]{:S(2)}) collective-permute-start(bf16[1040,128]{1,0:T(8,128)(2,1)S(1)} %get-tuple-element.12.refs_4_), channel_id=1, source_target_pairs={{0,48},{16,0},{32,16},{48,32},{1,49},{17,1},{33,17},{49,33},{2,50}... | collective-permute-start | bytes 798728 | tf_op jit(solution)/shard_map/ppermute | solution.py:251
  75.1 0.0 collective-permute-done.6.refs_8_
  75.1 0.0 collective-permute-start.7
  75.1 1.7 %collective-permute-start.8 = (bf16[1040,128]{1,0:T(8,128)(2,1)S(1)}, bf16[1040,128]{1,0:T(8,128)(2,1)S(1)}, u32[]{:S(2)}, u32[]{:S(2)}) collective-permute-start(bf16[1040,128]{1,0:T(8,128)(2,1)S(1)} %collective-permute-done.6.refs_8_), channel_id=1, source_target_pairs={{0,32},{16,48},{32,0},{48,16},{1,33},{17,49},{33,1},{49,17},{2,34}... | collective-permute-start | bytes 798728 | tf_op jit(solution)/shard_map/ppermute | solution.py:251
  76.9 0.0 collective-permute-done.3.refs_5_
  76.9 1.0 collective-permute-start.9
  77.9 0.0 collective-permute-done.4.refs_6_
  77.9 5.2 %collective-permute-done.5.refs_7_ = bf16[1040,128]{1,0:T(8,128)(2,1)S(1)} collective-permute-done((bf16[1040,128]{1,0:T(8,128)(2,1)S(1)}, bf16[1040,128]{1,0:T(8,128)(2,1)S(1)}, u32[]{:S(2)}, u32[]{:S(2)}) %collective-permute-start.5) | collective-permute-done | bytes 266272 | tf_op jit(solution)/shard_map/ppermute | solution.py:251
  83.1 5.6 %collective-permute-done.8.refs_10_ = bf16[1040,128]{1,0:T(8,128)(2,1)S(1)} collective-permute-done((bf16[1040,128]{1,0:T(8,128)(2,1)S(1)}, bf16[1040,128]{1,0:T(8,128)(2,1)S(1)}, u32[]{:S(2)}, u32[]{:S(2)}) %collective-permute-start.8) | collective-permute-done | bytes 266272 | tf_op jit(solution)/shard_map/ppermute | solution.py:251
  88.7 5.4 %collective-permute-done.9.refs_11_ = bf16[1040,128]{1,0:T(8,128)(2,1)S(1)} collective-permute-done((bf16[1040,128]{1,0:T(8,128)(2,1)S(1)}, bf16[1040,128]{1,0:T(8,128)(2,1)S(1)}, u32[]{:S(2)}, u32[]{:S(2)}) %collective-permute-start.9) | collective-permute-done | bytes 266272 | tf_op jit(solution)/shard_map/ppermute | solution.py:251
  94.2 0.7 copy-done.18
  94.9 13.5 %shard_map.46 = bf16[128,2176]{1,0:T(8,128)(2,1)} custom-call(s32[1]{0:T(128)S(6)} %copy.6.offset_ref, bf16[32,2048]{1,0:T(8,128)(2,1)} %copy-done.3, bf16[32,2048]{1,0:T(8,128)(2,1)} %copy-done.23, bf16[32,2048]{1,0:T(8,128)(2,1)} %copy-done.24, bf16[32,2048]{1,0:T(8,128)(2,1)} %copy-done.25, bf16[1040,128]{1,0:T(8,128)(2,1)} %copy-done.1, ...), custom_call_target="tpu_custom_call" | custom-call | tf_op jit(solution)/shard_map/pallas_call | solution.py:198
  108.4 24.8 %all_to_all.10 = bf16[16,8,2176]{2,1,0:T(8,128)(2,1)} all-to-all(bf16[16,8,2176]{2,1,0:T(8,128)(2,1)} %bitcast.19), channel_id=1, replica_groups=mesh['zl'=2,'y'=4,'x'=4,'zh'=2,'core'=2] {'x','zh','core'}, dimensions={0} | all-to-all | bytes 1114112 | tf_op jit(solution)/shard_map/all_to_all | solution.py:273
  133.1 3.9 %merge.1 = bf16[8,16384]{1,0:T(8,128)(2,1)} custom-call(bf16[4,4,8,2176]{3,2,1,0:T(8,128)(2,1)} %bitcast.20, bf16[4,4,8,2176]{3,2,1,0:T(8,128)(2,1)} %bitcast.18), custom_call_target="tpu_custom_call" | custom-call | tf_op jit(solution)/shard_map/merge/pallas_call | solution.py:239
  (57 shorter events, 0.1 us)
Async XLA Ops:
  1.9 4.1 %copy-start.19 = (bf16[32,4096]{1,0:T(8,128)(2,1)S(1)}, bf16[32,4096]{1,0:T(8,128)(2,1)}, u32[]{:S(2)}) copy-start(bf16[32,4096]{1,0:T(8,128)(2,1)} %param.4) | copy-start | bytes 786436
  2.3 33.1 %copy-start.2 = (bf16[1040,128]{1,0:T(8,128)(2,1)}, bf16[1040,128]{1,0:T(8,128)(2,1)S(1)}, u32[]{:S(2)}) copy-start(bf16[1040,128]{1,0:T(8,128)(2,1)S(1)} %get-tuple-element.11.refs_4_) | copy-start | bytes 798724
  2.3 70.5 %copy-start.1 = (bf16[1040,128]{1,0:T(8,128)(2,1)}, bf16[1040,128]{1,0:T(8,128)(2,1)S(1)}, u32[]{:S(2)}) copy-start(bf16[1040,128]{1,0:T(8,128)(2,1)S(1)} %get-tuple-element.12.refs_4_) | copy-start | bytes 798724
  2.3 14.1 %collective-permute-start.16 = (bf16[1040,128]{1,0:T(8,128)(2,1)S(1)}, bf16[1040,128]{1,0:T(8,128)(2,1)S(1)}, u32[]{:S(2)}, u32[]{:S(2)}) collective-permute-start(bf16[1040,128]{1,0:T(8,128)(2,1)S(1)} %get-tuple-element.11.refs_4_), channel_id=1, source_target_pairs={{0,64},{64,0},{1,65},{65,1},{2,66},{66,2},{3,67},{67,3},{4,68},{68... | collective-permute-start | bytes 798728 | tf_op jit(solution)/shard_map/ppermute | solution.py:251
  4.8 14.0 %collective-permute-start.13 = (bf16[1040,128]{1,0:T(8,128)(2,1)S(1)}, bf16[1040,128]{1,0:T(8,128)(2,1)S(1)}, u32[]{:S(2)}, u32[]{:S(2)}) collective-permute-start(bf16[1040,128]{1,0:T(8,128)(2,1)S(1)} %get-tuple-element.11.refs_4_), channel_id=1, source_target_pairs={{0,4},{4,8},{8,12},{12,0},{1,5},{5,9},{9,13},{13,1},{2,6},{6,10},{... | collective-permute-start | bytes 798728 | tf_op jit(solution)/shard_map/ppermute | solution.py:251
  6.1 29.3 %copy-start.4 = (bf16[32,2048]{1,0:T(8,128)(2,1)}, bf16[32,2048]{1,0:T(8,128)(2,1)S(1)}, u32[]{:S(2)}) copy-start(bf16[32,2048]{1,0:T(8,128)(2,1)S(1)} %get-tuple-element.9.refs_0_) | copy-start | bytes 393220
  6.1 60.4 %copy-start.3 = (bf16[32,2048]{1,0:T(8,128)(2,1)}, bf16[32,2048]{1,0:T(8,128)(2,1)S(1)}, u32[]{:S(2)}) copy-start(bf16[32,2048]{1,0:T(8,128)(2,1)S(1)} %get-tuple-element.10.refs_0_) | copy-start | bytes 393220
  6.1 5.5 %collective-permute-start.10 = (bf16[32,2048]{1,0:T(8,128)(2,1)S(1)}, bf16[32,2048]{1,0:T(8,128)(2,1)S(1)}, u32[]{:S(2)}, u32[]{:S(2)}) collective-permute-start(bf16[32,2048]{1,0:T(8,128)(2,1)S(1)} %get-tuple-element.9.refs_0_), channel_id=1, source_target_pairs={{0,16},{16,32},{32,48},{48,0},{1,17},{17,33},{33,49},{49,1},{2,18}... | collective-permute-start | bytes 393224 | tf_op jit(solution)/shard_map/ppermute | solution.py:251
  7.5 7.5 %collective-permute-start.11 = (bf16[32,2048]{1,0:T(8,128)(2,1)S(1)}, bf16[32,2048]{1,0:T(8,128)(2,1)S(1)}, u32[]{:S(2)}, u32[]{:S(2)}) collective-permute-start(bf16[32,2048]{1,0:T(8,128)(2,1)S(1)} %get-tuple-element.9.refs_0_), channel_id=1, source_target_pairs={{0,32},{16,48},{32,0},{48,16},{1,33},{17,49},{33,1},{49,17},{2,34}... | collective-permute-start | bytes 393224 | tf_op jit(solution)/shard_map/ppermute | solution.py:251
  10.1 6.3 %collective-permute-start.12 = (bf16[32,2048]{1,0:T(8,128)(2,1)S(1)}, bf16[32,2048]{1,0:T(8,128)(2,1)S(1)}, u32[]{:S(2)}, u32[]{:S(2)}) collective-permute-start(bf16[32,2048]{1,0:T(8,128)(2,1)S(1)} %get-tuple-element.9.refs_0_), channel_id=1, source_target_pairs={{0,48},{16,0},{32,16},{48,32},{1,49},{17,1},{33,17},{49,33},{2,50}... | collective-permute-start | bytes 393224 | tf_op jit(solution)/shard_map/ppermute | solution.py:251
  11.6 23.9 %copy-start.20 = (bf16[32,2048]{1,0:T(8,128)(2,1)}, bf16[32,2048]{1,0:T(8,128)(2,1)S(1)}, u32[]{:S(2)}) copy-start(bf16[32,2048]{1,0:T(8,128)(2,1)S(1)} %collective-permute-done.10.refs_1_) | copy-start | bytes 393220
  11.6 8.5 %collective-permute-start.14 = (bf16[1040,128]{1,0:T(8,128)(2,1)S(1)}, bf16[1040,128]{1,0:T(8,128)(2,1)S(1)}, u32[]{:S(2)}, u32[]{:S(2)}) collective-permute-start(bf16[1040,128]{1,0:T(8,128)(2,1)S(1)} %get-tuple-element.11.refs_4_), channel_id=1, source_target_pairs={{0,8},{4,12},{8,0},{12,4},{1,9},{5,13},{9,1},{13,5},{2,10},{6,14},... | collective-permute-start | bytes 798728 | tf_op jit(solution)/shard_map/ppermute | solution.py:251
  14.9 20.5 %copy-start.21 = (bf16[32,2048]{1,0:T(8,128)(2,1)}, bf16[32,2048]{1,0:T(8,128)(2,1)S(1)}, u32[]{:S(2)}) copy-start(bf16[32,2048]{1,0:T(8,128)(2,1)S(1)} %collective-permute-done.11.refs_2_) | copy-start | bytes 393220
  14.9 10.6 %collective-permute-start.15 = (bf16[1040,128]{1,0:T(8,128)(2,1)S(1)}, bf16[1040,128]{1,0:T(8,128)(2,1)S(1)}, u32[]{:S(2)}, u32[]{:S(2)}) collective-permute-start(bf16[1040,128]{1,0:T(8,128)(2,1)S(1)} %get-tuple-element.11.refs_4_), channel_id=1, source_target_pairs={{0,12},{4,0},{8,4},{12,8},{1,13},{5,1},{9,5},{13,9},{2,14},{6,2},{... | collective-permute-start | bytes 798728 | tf_op jit(solution)/shard_map/ppermute | solution.py:251
  16.4 19.0 %copy-start.7 = (bf16[1040,128]{1,0:T(8,128)(2,1)}, bf16[1040,128]{1,0:T(8,128)(2,1)S(1)}, u32[]{:S(2)}) copy-start(bf16[1040,128]{1,0:T(8,128)(2,1)S(1)} %collective-permute-done.16.refs_8_) | copy-start | bytes 798724
  16.4 9.9 %collective-permute-start.17 = (bf16[1040,128]{1,0:T(8,128)(2,1)S(1)}, bf16[1040,128]{1,0:T(8,128)(2,1)S(1)}, u32[]{:S(2)}, u32[]{:S(2)}) collective-permute-start(bf16[1040,128]{1,0:T(8,128)(2,1)S(1)} %collective-permute-done.16.refs_8_), channel_id=1, source_target_pairs={{0,4},{4,8},{8,12},{12,0},{1,5},{5,9},{9,13},{13,1},{2,6},{6,10},{... | collective-permute-start | bytes 798728 | tf_op jit(solution)/shard_map/ppermute | solution.py:251
  16.4 3.6 %copy-start.22 = (bf16[32,2048]{1,0:T(8,128)(2,1)}, bf16[32,2048]{1,0:T(8,128)(2,1)S(1)}, u32[]{:S(2)}) copy-start(bf16[32,2048]{1,0:T(8,128)(2,1)S(1)} %collective-permute-done.12.refs_3_) | copy-start | bytes 393220
  16.4 15.1 %collective-permute-start.18 = (bf16[1040,128]{1,0:T(8,128)(2,1)S(1)}, bf16[1040,128]{1,0:T(8,128)(2,1)S(1)}, u32[]{:S(2)}, u32[]{:S(2)}) collective-permute-start(bf16[1040,128]{1,0:T(8,128)(2,1)S(1)} %collective-permute-done.16.refs_8_), channel_id=1, source_target_pairs={{0,8},{4,12},{8,0},{12,4},{1,9},{5,13},{9,1},{13,5},{2,10},{6,14},... | collective-permute-start | bytes 798728 | tf_op jit(solution)/shard_map/ppermute | solution.py:251
  18.9 16.5 %copy-start.8 = (bf16[1040,128]{1,0:T(8,128)(2,1)}, bf16[1040,128]{1,0:T(8,128)(2,1)S(1)}, u32[]{:S(2)}) copy-start(bf16[1040,128]{1,0:T(8,128)(2,1)S(1)} %collective-permute-done.13.refs_5_) | copy-start | bytes 798724
  18.9 16.5 %collective-permute-start.19 = (bf16[1040,128]{1,0:T(8,128)(2,1)S(1)}, bf16[1040,128]{1,0:T(8,128)(2,1)S(1)}, u32[]{:S(2)}, u32[]{:S(2)}) collective-permute-start(bf16[1040,128]{1,0:T(8,128)(2,1)S(1)} %collective-permute-done.16.refs_8_), channel_id=1, source_target_pairs={{0,12},{4,0},{8,4},{12,8},{1,13},{5,1},{9,5},{13,9},{2,14},{6,2},{... | collective-permute-start | bytes 798728 | tf_op jit(solution)/shard_map/ppermute | solution.py:251
  20.0 15.4 %copy-start.9 = (bf16[1040,128]{1,0:T(8,128)(2,1)}, bf16[1040,128]{1,0:T(8,128)(2,1)S(1)}, u32[]{:S(2)}) copy-start(bf16[1040,128]{1,0:T(8,128)(2,1)S(1)} %collective-permute-done.14.refs_6_) | copy-start | bytes 798724
  20.0 55.1 %collective-permute-start.6 = (bf16[1040,128]{1,0:T(8,128)(2,1)S(1)}, bf16[1040,128]{1,0:T(8,128)(2,1)S(1)}, u32[]{:S(2)}, u32[]{:S(2)}) collective-permute-start(bf16[1040,128]{1,0:T(8,128)(2,1)S(1)} %get-tuple-element.12.refs_4_), channel_id=1, source_target_pairs={{0,64},{64,0},{1,65},{65,1},{2,66},{66,2},{3,67},{67,3},{4,68},{68... | collective-permute-start | bytes 798728 | tf_op jit(solution)/shard_map/ppermute | solution.py:251
  25.5 9.9 %copy-start.10 = (bf16[1040,128]{1,0:T(8,128)(2,1)}, bf16[1040,128]{1,0:T(8,128)(2,1)S(1)}, u32[]{:S(2)}) copy-start(bf16[1040,128]{1,0:T(8,128)(2,1)S(1)} %collective-permute-done.15.refs_7_) | copy-start | bytes 798724
  25.5 51.3 %collective-permute-start.3 = (bf16[1040,128]{1,0:T(8,128)(2,1)S(1)}, bf16[1040,128]{1,0:T(8,128)(2,1)S(1)}, u32[]{:S(2)}, u32[]{:S(2)}) collective-permute-start(bf16[1040,128]{1,0:T(8,128)(2,1)S(1)} %get-tuple-element.12.refs_4_), channel_id=1, source_target_pairs={{0,16},{16,32},{32,48},{48,0},{1,17},{17,33},{33,49},{49,1},{2,18}... | collective-permute-start | bytes 798728 | tf_op jit(solution)/shard_map/ppermute | solution.py:251
  26.4 9.1 %copy-start.12 = (bf16[1040,128]{1,0:T(8,128)(2,1)}, bf16[1040,128]{1,0:T(8,128)(2,1)S(1)}, u32[]{:S(2)}) copy-start(bf16[1040,128]{1,0:T(8,128)(2,1)S(1)} %collective-permute-done.17.refs_9_) | copy-start | bytes 798724
  31.6 3.9 %copy-start.14 = (bf16[1040,128]{1,0:T(8,128)(2,1)}, bf16[1040,128]{1,0:T(8,128)(2,1)S(1)}, u32[]{:S(2)}) copy-start(bf16[1040,128]{1,0:T(8,128)(2,1)S(1)} %collective-permute-done.18.refs_10_) | copy-start | bytes 798724
  35.5 0.7 copy-start.16
  55.2 53.2 %all-to-all-start.1 = ((bf16[16,8,2176]{2,1,0:T(8,128)(2,1)}), bf16[16,8,2176]{2,1,0:T(8,128)(2,1)S(1)}, u32[]{:S(2)}, u32[]{:S(2)}) async-start(bf16[16,8,2176]{2,1,0:T(8,128)(2,1)} %bitcast.17), calls=%async_computation.1 | async-start | bytes 1114112 | tf_op jit(solution)/shard_map/all_to_all | solution.py:273
  62.7 6.1 %collective-permute-start = (bf16[32,2048]{1,0:T(8,128)(2,1)S(1)}, bf16[32,2048]{1,0:T(8,128)(2,1)S(1)}, u32[]{:S(2)}, u32[]{:S(2)}) collective-permute-start(bf16[32,2048]{1,0:T(8,128)(2,1)S(1)} %get-tuple-element.10.refs_0_), channel_id=1, source_target_pairs={{0,4},{4,8},{8,12},{12,0},{1,5},{5,9},{9,13},{13,1},{2,6},{6,10},{... | collective-permute-start | bytes 393224 | tf_op jit(solution)/shard_map/ppermute | solution.py:251
  64.6 8.2 %collective-permute-start.1 = (bf16[32,2048]{1,0:T(8,128)(2,1)S(1)}, bf16[32,2048]{1,0:T(8,128)(2,1)S(1)}, u32[]{:S(2)}, u32[]{:S(2)}) collective-permute-start(bf16[32,2048]{1,0:T(8,128)(2,1)S(1)} %get-tuple-element.10.refs_0_), channel_id=1, source_target_pairs={{0,8},{4,12},{8,0},{12,4},{1,9},{5,13},{9,1},{13,5},{2,10},{6,14},... | collective-permute-start | bytes 393224 | tf_op jit(solution)/shard_map/ppermute | solution.py:251
  66.5 8.6 %collective-permute-start.2 = (bf16[32,2048]{1,0:T(8,128)(2,1)S(1)}, bf16[32,2048]{1,0:T(8,128)(2,1)S(1)}, u32[]{:S(2)}, u32[]{:S(2)}) collective-permute-start(bf16[32,2048]{1,0:T(8,128)(2,1)S(1)} %get-tuple-element.10.refs_0_), channel_id=1, source_target_pairs={{0,12},{4,0},{8,4},{12,8},{1,13},{5,1},{9,5},{13,9},{2,14},{6,2},{... | collective-permute-start | bytes 393224 | tf_op jit(solution)/shard_map/ppermute | solution.py:251
  68.8 25.3 %copy-start.23 = (bf16[32,2048]{1,0:T(8,128)(2,1)}, bf16[32,2048]{1,0:T(8,128)(2,1)S(1)}, u32[]{:S(2)}) copy-start(bf16[32,2048]{1,0:T(8,128)(2,1)S(1)} %collective-permute-done.refs_1_) | copy-start | bytes 393220
  68.8 9.1 %collective-permute-start.4 = (bf16[1040,128]{1,0:T(8,128)(2,1)S(1)}, bf16[1040,128]{1,0:T(8,128)(2,1)S(1)}, u32[]{:S(2)}, u32[]{:S(2)}) collective-permute-start(bf16[1040,128]{1,0:T(8,128)(2,1)S(1)} %get-tuple-element.12.refs_4_), channel_id=1, source_target_pairs={{0,32},{16,48},{32,0},{48,16},{1,33},{17,49},{33,1},{49,17},{2,34}... | collective-permute-start | bytes 798728 | tf_op jit(solution)/shard_map/ppermute | solution.py:251
  72.8 21.3 %copy-start.24 = (bf16[32,2048]{1,0:T(8,128)(2,1)}, bf16[32,2048]{1,0:T(8,128)(2,1)S(1)}, u32[]{:S(2)}) copy-start(bf16[32,2048]{1,0:T(8,128)(2,1)S(1)} %collective-permute-done.1.refs_2_) | copy-start | bytes 393220
  72.8 10.4 %collective-permute-start.5 = (bf16[1040,128]{1,0:T(8,128)(2,1)S(1)}, bf16[1040,128]{1,0:T(8,128)(2,1)S(1)}, u32[]{:S(2)}, u32[]{:S(2)}) collective-permute-start(bf16[1040,128]{1,0:T(8,128)(2,1)S(1)} %get-tuple-element.12.refs_4_), channel_id=1, source_target_pairs={{0,48},{16,0},{32,16},{48,32},{1,49},{17,1},{33,17},{49,33},{2,50}... | collective-permute-start | bytes 798728 | tf_op jit(solution)/shard_map/ppermute | solution.py:251
  75.1 19.0 %copy-start.5 = (bf16[1040,128]{1,0:T(8,128)(2,1)}, bf16[1040,128]{1,0:T(8,128)(2,1)S(1)}, u32[]{:S(2)}) copy-start(bf16[1040,128]{1,0:T(8,128)(2,1)S(1)} %collective-permute-done.6.refs_8_) | copy-start | bytes 798724
  75.1 8.0 %collective-permute-start.7 = (bf16[1040,128]{1,0:T(8,128)(2,1)S(1)}, bf16[1040,128]{1,0:T(8,128)(2,1)S(1)}, u32[]{:S(2)}, u32[]{:S(2)}) collective-permute-start(bf16[1040,128]{1,0:T(8,128)(2,1)S(1)} %collective-permute-done.6.refs_8_), channel_id=1, source_target_pairs={{0,16},{16,32},{32,48},{48,0},{1,17},{17,33},{33,49},{49,1},{2,18}... | collective-permute-start | bytes 798728 | tf_op jit(solution)/shard_map/ppermute | solution.py:251
  75.1 19.0 %copy-start.25 = (bf16[32,2048]{1,0:T(8,128)(2,1)}, bf16[32,2048]{1,0:T(8,128)(2,1)S(1)}, u32[]{:S(2)}) copy-start(bf16[32,2048]{1,0:T(8,128)(2,1)S(1)} %collective-permute-done.2.refs_3_) | copy-start | bytes 393220
  75.1 13.6 %collective-permute-start.8 = (bf16[1040,128]{1,0:T(8,128)(2,1)S(1)}, bf16[1040,128]{1,0:T(8,128)(2,1)S(1)}, u32[]{:S(2)}, u32[]{:S(2)}) collective-permute-start(bf16[1040,128]{1,0:T(8,128)(2,1)S(1)} %collective-permute-done.6.refs_8_), channel_id=1, source_target_pairs={{0,32},{16,48},{32,0},{48,16},{1,33},{17,49},{33,1},{49,17},{2,34}... | collective-permute-start | bytes 798728 | tf_op jit(solution)/shard_map/ppermute | solution.py:251
  76.9 17.2 %copy-start.6 = (bf16[1040,128]{1,0:T(8,128)(2,1)}, bf16[1040,128]{1,0:T(8,128)(2,1)S(1)}, u32[]{:S(2)}) copy-start(bf16[1040,128]{1,0:T(8,128)(2,1)S(1)} %collective-permute-done.3.refs_5_) | copy-start | bytes 798724
  76.9 17.2 %collective-permute-start.9 = (bf16[1040,128]{1,0:T(8,128)(2,1)S(1)}, bf16[1040,128]{1,0:T(8,128)(2,1)S(1)}, u32[]{:S(2)}, u32[]{:S(2)}) collective-permute-start(bf16[1040,128]{1,0:T(8,128)(2,1)S(1)} %collective-permute-done.6.refs_8_), channel_id=1, source_target_pairs={{0,48},{16,0},{32,16},{48,32},{1,49},{17,1},{33,17},{49,33},{2,50}... | collective-permute-start | bytes 798728 | tf_op jit(solution)/shard_map/ppermute | solution.py:251
  77.9 16.2 %copy-start.11 = (bf16[1040,128]{1,0:T(8,128)(2,1)}, bf16[1040,128]{1,0:T(8,128)(2,1)S(1)}, u32[]{:S(2)}) copy-start(bf16[1040,128]{1,0:T(8,128)(2,1)S(1)} %collective-permute-done.4.refs_6_) | copy-start | bytes 798724
  83.1 11.0 %copy-start.13 = (bf16[1040,128]{1,0:T(8,128)(2,1)}, bf16[1040,128]{1,0:T(8,128)(2,1)S(1)}, u32[]{:S(2)}) copy-start(bf16[1040,128]{1,0:T(8,128)(2,1)S(1)} %collective-permute-done.5.refs_7_) | copy-start | bytes 798724
  83.1 11.0 %copy-start.15 = (bf16[1040,128]{1,0:T(8,128)(2,1)}, bf16[1040,128]{1,0:T(8,128)(2,1)S(1)}, u32[]{:S(2)}) copy-start(bf16[1040,128]{1,0:T(8,128)(2,1)S(1)} %collective-permute-done.7.refs_9_) | copy-start | bytes 798724
  88.7 5.4 %copy-start.17 = (bf16[1040,128]{1,0:T(8,128)(2,1)}, bf16[1040,128]{1,0:T(8,128)(2,1)S(1)}, u32[]{:S(2)}) copy-start(bf16[1040,128]{1,0:T(8,128)(2,1)S(1)} %collective-permute-done.8.refs_10_) | copy-start | bytes 798724
  94.2 0.7 copy-start.18
  108.4 24.8 %copy-start = (bf16[16,8,2176]{2,1,0:T(8,128)(2,1)}, bf16[16,8,2176]{2,1,0:T(8,128)(2,1)S(1)}, u32[]{:S(2)}) copy-start(bf16[16,8,2176]{2,1,0:T(8,128)(2,1)S(1)} %all-to-all-done.1) | copy-start | bytes 1671172
